TPU v7x, 32 devices: a whole 2x2x4 slice. The times are simulated.
32 devices in a mesh: dp: 8 (over z, y), tensor: 4 (over x, core).
Axes of the slice: x: 2, y: 2, z: 4, core: 2. Of those that a mesh axis runs over, the one named last changes fastest.
Arguments:
- query_act: bfloat16 [8, 1024, 1024], P('dp', None, 'tensor'), may hold values from -6 to 6
- rotated_keys: bfloat16 [8, 1024, 256], P('dp'), may hold values from -6 to 6
- value_input: bfloat16 [8, 1024, 256], P('dp'), may hold values from -6 to 6
- grad_out: bfloat16 [8, 1024, 8192], P('dp', 'tensor'), may hold values from -6 to 6
- out_weight: bfloat16 [1024, 8192], P('tensor', 'dp'), may hold values from -0.1875 to 0.1875
- doc_lengths: int32 [8, 4], P('dp'), may hold values from 1 to 512, 1024 in all within a row
Outputs:
- query_grad: bfloat16 [8, 1024, 1024], P('dp', None, 'tensor')
- key_gradient: bfloat16 [8, 4, 512, 128], P('dp', 'tensor')
- value_gradient: bfloat16 [8, 4, 512, 128], P('dp', 'tensor')
- weight_grad: float32 [1024, 8192], P('tensor', 'dp')
All inputs are finite; a program needn't handle non-finite values.
Results may differ from a plain program's by a relative error of at most 0.015.
The roundings to bfloat16 on the way count: a program that leaves them out, or rounds other values in their place, can miss the bound.
Values may be sent and summed in bfloat16 or wider, within the bound.
A program may use at most 128 MiB of HBM per device.

v0:
```python
import jax
import jax.numpy as jnp
from jax import lax
from jax.sharding import PartitionSpec as P

HEAD_SIZE = 128


def swapped(value, axis, apart):
    mask = 2**apart
    pairs = [(source, source ^ mask) for source in range(lax.axis_size(axis))]
    return lax.ppermute(value, axis, pairs)


def shards(query_act, rotated_keys, value_input, grad_out, out_weight, doc_lengths):
    score_scale = HEAD_SIZE ** (-0.5)
    tensor_index = lax.axis_index("tensor")
    kv_group = tensor_index // 2
    own_half = tensor_index % 2
    seq_len = query_act.shape[1]
    head_count = query_act.shape[2] // HEAD_SIZE
    query_heads = query_act[0].reshape(seq_len, head_count, HEAD_SIZE).transpose(1, 0, 2)
    key_rows = lax.dynamic_slice_in_dim(rotated_keys[0], kv_group * HEAD_SIZE, HEAD_SIZE, 1)
    value_rows = lax.dynamic_slice_in_dim(value_input[0], kv_group * HEAD_SIZE, HEAD_SIZE, 1)
    doc_ends = jnp.cumsum(doc_lengths[0])
    positions = jnp.arange(seq_len, dtype=jnp.int32)
    doc_ids = jnp.sum((positions[:, None] >= doc_ends[None, :]).astype(jnp.int32), axis=1)
    block_rows = min(512, seq_len)
    block_count = seq_len // block_rows
    full_weight = lax.all_gather(out_weight, "dp", axis=1, tiled=True)

    def key_reach():
        return seq_len

    def masked_scores(block_idx, key_span):
        first = block_idx * block_rows
        query_block = query_heads[:, first : first + block_rows]
        scores = (
            jnp.einsum("hqd,kd->hqk", query_block, key_rows, preferred_element_type=jnp.float32)
            * score_scale
        )
        allowed = (positions[None, :key_span] <= positions[first : first + block_rows, None]) & (
            doc_ids[None, :key_span] == doc_ids[first : first + block_rows, None]
        )
        return jnp.where(allowed[None], scores, -jnp.inf)

    totals_list = []
    outputs_list = []
    for block_idx in range(block_count):
        key_span = key_reach()
        scores = masked_scores(block_idx, key_span)
        row_max = jnp.max(scores, axis=-1, keepdims=True)
        log_total = row_max + jnp.log(jnp.sum(jnp.exp(scores - row_max), axis=-1, keepdims=True))
        prob_bf16 = jnp.exp(scores - log_total).astype(jnp.bfloat16)
        outputs_list.append(
            jnp.einsum(
                "hqk,kd->hqd", prob_bf16, value_rows, preferred_element_type=jnp.float32
            ).astype(jnp.bfloat16)
        )
        totals_list.append(log_total)
    attn_out = jnp.concatenate(outputs_list, axis=1)
    out_flat = attn_out.transpose(1, 0, 2).reshape(seq_len, head_count * HEAD_SIZE)
    local_rows = grad_out[0]
    gathered = lax.all_gather(local_rows, "tensor", axis=0, tiled=True)
    out_grad = jnp.einsum(
        "sd,hd->sh", gathered, full_weight, preferred_element_type=jnp.float32
    ).astype(jnp.bfloat16)
    weight_part = jnp.einsum("sh,sd->hd", out_flat, gathered, preferred_element_type=jnp.float32)
    weight_grad = lax.psum_scatter(weight_part, "dp", scatter_dimension=1, tiled=True)
    grad_heads = out_grad.reshape(seq_len, head_count, HEAD_SIZE).transpose(1, 0, 2)
    key_accum = jnp.zeros((seq_len, HEAD_SIZE), jnp.float32)
    value_accum = jnp.zeros((seq_len, HEAD_SIZE), jnp.float32)
    query_list = []
    for block_idx in range(block_count):
        key_span = key_reach()
        first = block_idx * block_rows
        scores = masked_scores(block_idx, key_span)
        prob_block = jnp.exp(scores - totals_list[block_idx])
        prob_bf16 = prob_block.astype(jnp.bfloat16)
        grad_block = grad_heads[:, first : first + block_rows]
        out_block = attn_out[:, first : first + block_rows]
        query_block = query_heads[:, first : first + block_rows]
        dprobs = jnp.einsum(
            "hqd,kd->hqk", grad_block, value_rows, preferred_element_type=jnp.float32
        )
        row_delta = jnp.sum(
            grad_block.astype(jnp.float32) * out_block.astype(jnp.float32), axis=-1, keepdims=True
        )
        score_gradient = (prob_block * (dprobs - row_delta) * score_scale).astype(jnp.bfloat16)
        query_list.append(
            jnp.einsum(
                "hqk,kd->hqd", score_gradient, key_rows, preferred_element_type=jnp.float32
            ).astype(jnp.bfloat16)
        )
        key_accum = key_accum.at[:key_span].add(
            jnp.einsum(
                "hqk,hqd->kd", score_gradient, query_block, preferred_element_type=jnp.float32
            )
        )
        value_accum = value_accum.at[:key_span].add(
            jnp.einsum("hqk,hqd->kd", prob_bf16, grad_block, preferred_element_type=jnp.float32)
        )
    query_grad = (
        jnp.concatenate(query_list, axis=1)
        .transpose(1, 0, 2)
        .reshape(1, seq_len, head_count * HEAD_SIZE)
    )
    half_rows = seq_len // 2
    other_start = (1 - own_half) * half_rows
    outgoing = (
        lax.dynamic_slice_in_dim(key_accum, other_start, half_rows, 0),
        lax.dynamic_slice_in_dim(value_accum, other_start, half_rows, 0),
    )
    partner = swapped((outgoing[0], outgoing[1]), "tensor", 0)
    key_mine = lax.dynamic_slice_in_dim(key_accum, own_half * half_rows, half_rows, 0) + partner[0]
    value_mine = (
        lax.dynamic_slice_in_dim(value_accum, own_half * half_rows, half_rows, 0) + partner[1]
    )
    key_gradient = key_mine.astype(jnp.bfloat16).reshape(1, 1, half_rows, HEAD_SIZE)
    value_gradient = value_mine.astype(jnp.bfloat16).reshape(1, 1, half_rows, HEAD_SIZE)
    return (query_grad, key_gradient, value_gradient, weight_grad)


def solution(mesh):
    placed = (
        P("dp", None, "tensor"),
        P("dp", None, None),
        P("dp", None, None),
        P("dp", "tensor", None),
        P("tensor", "dp"),
        P("dp", None),
    )
    return jax.shard_map(
        shards,
        mesh=mesh,
        in_specs=placed,
        out_specs=(
            P("dp", None, "tensor"),
            P("dp", "tensor", None, None),
            P("dp", "tensor", None, None),
            P("tensor", "dp"),
        ),
        check_vma=False,
    )
```

profile of v0, /device:TPU:0, one launch (start us, length us, event | category | flops | bytes accessed | tf_op | source)
XLA Modules:
  0.0 374.6 jit_solution(8681585686457070649)
XLA Ops:
  7.2 0.0 copy-start
  7.2 0.0 copy-start.10
  7.2 0.0 copy-start.5
  7.2 0.0 copy-start.8
  7.2 0.0 all-gather.4.cloned.1.call-start
  7.3 0.7 all-gather.4.cloned.1.call-update
  7.9 0.0 all-gather.6.cloned.1.call-start
  8.0 0.7 all-gather.6.cloned.1.call-update
  8.7 0.0 reduce-scatter.2.cloned.1.call-start
  8.8 0.0 copy-done.10
  8.8 0.2 reduce-window.8
  9.0 0.0 copy-done.5
  9.0 0.2 copy.29
  9.2 0.3 copy.30
  9.5 0.1 convert_reduce_fusion
  9.6 0.9 fusion.9
  10.5 0.0 copy-done.8
  10.5 0.9 fusion.7
  11.4 0.0 copy-start.1
  11.4 0.9 fusion.6
  12.4 0.0 copy-start.3
  12.4 2.2 exponential_reduce_fusion
  14.5 0.1 copy-done.3
  14.7 0.0 copy-done.1
  14.7 0.0 copy-done
  14.7 1.6 convolution_convert_fusion.1
  16.2 69.5 %all-gather.4.cloned.1.call-done = bf16[256,8192]{1,0:T(8,128)(2,1)} async-done(((bf16[256,1024]{1,0:T(8,128)(2,1)}), bf16[256,8192]{1,0:T(8,128)(2,1)}) %all-gather.4.cloned.1.call-update) | async-done | bytes 4194320 | tf_op jit(solution)/shard_map/all_gather | solution.py:30
  85.7 106.0 %all-gather.6.cloned.1.call-done = bf16[1,1024,8192]{2,1,0:T(8,128)(2,1)} async-done(((bf16[1,256,8192]{2,1,0:T(8,128)(2,1)}), bf16[1,1024,8192]{2,1,0:T(8,128)(2,1)}) %all-gather.6.cloned.1.call-update) | async-done | bytes 16777232 | tf_op jit(solution)/shard_map/all_gather | solution.py:64
  191.8 11.5 %fusion.10 = bf16[1024,256]{0,1:T(8,128)(2,1)S(1)} fusion(bf16[256,8192]{1,0:T(8,128)(2,1)} %all-gather.4.cloned.1.call-done, bf16[1,1024,8192]{2,1,0:T(8,128)(2,1)} %all-gather.6.cloned.1.call-done), kind=kOutput, calls=%fused_computation.20 | convolution fusion | flops 4295229440 | bytes 21495808 | tf_op jit(solution)/shard_map/sd,hd->sh/dot_general | solution.py:65
  203.2 0.3 copy.31
  203.5 0.0 copy-start.6
  203.5 3.8 %multiply_reduce_fusion.1 = (f32[2,512]{1,0:T(2,128)S(1)}, f32[2,512]{1,0:T(2,128)S(1)}, bf16[2,512,128]{2,1,0:T(8,128)(2,1)S(1)}) fusion(bf16[2,1024,128]{2,1,0:T(8,128)(2,1)S(1)} %bitcast.100, bf16[2,512,128]{2,1,0:T(8,128)(2,1)S(1)} %convolution_convert_fusion.1, bf16[1,1024,256]{2,1,0:T(8,128)(2,1)S(1)} %copy-done, s32[]{:T(128)S(6)} %select_n.33, ...), kind=kOutput, calls=%fused_computation.34 | convolution fusion | flops 273807360 | bytes 6041604 | tf_op jit(solution)/shard_map/hqk,kd->hqd/dot_general | solution.py:56
  207.3 0.0 copy-done.6
  207.4 0.2 copy.39
  207.6 12.5 %fusion = f32[256,8192]{1,0:T(8,128)} fusion(bf16[1024,256]{0,1:T(8,128)(2,1)S(1)} %bitcast.93, bf16[1,1024,8192]{2,1,0:T(8,128)(2,1)} %all-gather.6.cloned.1.call-done), kind=kOutput, calls=%fused_computation | convolution fusion | flops 4294967296 | bytes 25690112 | tf_op jit(solution)/shard_map/sh,sd->hd/dot_general | solution.py:68
  220.1 0.0 copy-start.7
  220.1 0.0 reduce-scatter.2.cloned.1.call-update
  220.1 1.0 copy-done.7
  221.1 0.0 copy-start.4
  221.1 4.0 %multiply_convert_fusion = bf16[2,512,1024]{1,2,0:T(8,128)(2,1)S(1)} fusion(f32[1024,2,512]{2,0,1:T(8,128)} %copy-done.1, f32[2,512]{1,0:T(2,128)S(1)} %get-tuple-element.93, f32[2,512]{1,0:T(2,128)S(1)} %log_add_fusion, pred[512,1024]{0,1:T(8,128)(4,1)S(1)} %get-tuple-element.94, bf16[2,1024,128]{2,1,0:T(8,128)(2,1)S(1)} %bitcast.101, ...), kind=kOutput, calls=%fused_computation.6 | convolution fusion | flops 275775488 | bytes 7348228 | tf_op jit(solution)/shard_map/hqd,kd->hqk/dot_general | solution.py:83
  225.1 0.7 convolution_bitcast_fusion.2
  225.8 0.0 copy-done.4
  225.8 0.0 copy-start.9
  225.8 1.7 multiply_convert_fusion.1
  227.5 0.0 copy-start.2
  227.5 0.7 fusion.13
  228.3 0.3 collective-permute-start
  228.6 0.0 copy-done.9
  228.6 0.8 convolution_convert_fusion
  229.4 0.4 copy-done.2
  229.8 1.1 convolution_bitcast_fusion
  230.8 1.3 fusion.14
  232.1 0.8 convolution_convert_fusion.2
  232.9 0.3 collective-permute-start.1
  233.3 0.2 copy.38
  233.5 1.0 copy.40
  234.5 0.0 collective-permute-done
  234.5 0.7 fusion.41
  235.2 0.0 collective-permute-done.1
  235.2 1.6 fusion.42
  236.8 131.3 %reduce-scatter.2.cloned.1.call-done = f32[256,1024]{1,0:T(8,128)} async-done(((f32[256,8192]{1,0:T(8,128)}), f32[256,1024]{1,0:T(8,128)}) %reduce-scatter.2.cloned.1.call-update) | async-done | bytes 1048592 | tf_op jit(solution)/shard_map/reduce_scatter | solution.py:69
  (11 shorter events, 0.2 us)
Async XLA Ops:
  7.2 7.5 %copy-start = (bf16[1,1024,256]{2,1,0:T(8,128)(2,1)S(1)}, bf16[1,1024,256]{2,1,0:T(8,128)(2,1)}, u32[]{:S(2)}) copy-start(bf16[1,1024,256]{2,1,0:T(8,128)(2,1)} %param.24) | copy-start | bytes 1572868
  7.2 1.6 copy-start.10
  7.2 1.8 copy-start.5
  7.2 3.3 copy-start.8
  7.2 78.5 %all-gather.4.cloned.1.call-start = ((), (), s32[]{:S(2)}) async-start(), calls=%async_computation.1 | async-start | bytes 4718592 | tf_op jit(solution)/shard_map/all_gather | solution.py:30
  7.9 183.8 %all-gather.6.cloned.1.call-start = ((), (), s32[]{:S(2)}) async-start(), calls=%async_computation.3 | async-start | bytes 20971520 | tf_op jit(solution)/shard_map/all_gather | solution.py:64
  8.7 359.4 %reduce-scatter.2.cloned.1.call-start = ((), (), s32[]{:S(2)}) async-start(), calls=%async_computation.2 | async-start | bytes 9437184 | tf_op jit(solution)/shard_map/reduce_scatter | solution.py:69
  11.4 3.2 copy-start.1
  12.4 2.3 copy-start.3
  203.5 3.8 %copy-start.6 = (bf16[1024,2,128]{2,0,1:T(8,128)(2,1)}, bf16[1024,2,128]{2,0,1:T(8,128)(2,1)S(1)}, u32[]{:S(2)}) copy-start(bf16[1024,2,128]{2,0,1:T(8,128)(2,1)S(1)} %copy.31) | copy-start | bytes 1572868
  220.1 1.0 copy-start.7
  221.1 4.7 %copy-start.4 = (f32[1024,2,512]{2,0,1:T(8,128)S(1)}, f32[1024,2,512]{2,0,1:T(8,128)}, u32[]{:S(2)}) copy-start(f32[1024,2,512]{2,0,1:T(8,128)} %copy-done.3) | copy-start | bytes 12582916
  225.8 2.8 copy-start.9
  227.5 2.3 copy-start.2
  228.3 6.2 %collective-permute-start = (f32[512,128]{1,0:T(8,128)S(1)}, f32[512,128]{1,0:T(8,128)S(1)}, u32[]{:S(2)}, u32[]{:S(2)}) collective-permute-start(f32[512,128]{1,0:T(8,128)S(1)} %constant_dynamic-slice_fusion.1), channel_id=1, source_target_pairs={{0,1},{1,0},{2,3},{3,2},{4,5},{5,4},{6,7},{7,6},{8,9},{9,8},{10,11... | collective-permute-start | bytes 786440 | tf_op jit(solution)/shard_map/ppermute | solution.py:12
  232.9 2.3 collective-permute-start.1
Sparse Core Ops, SparseCore 0:
  10.2 75.4 all-gather.3
  87.3 104.4 all-gather.5
  220.2 147.8 reduce-scatter.1
where the time goes:
time: 375 us
  waiting for transfers between devices  308 us (82%)
  matrix products  42.1 us (11%)
  between operations  14.1 us (4%)
  other arithmetic  5.72 us (2%)
  local copies, waits for them, and re-layouts  3.8 us (1%)
    reduce_scatter x1, waiting for transfers between devices, shards(): lax.psum_scatter(weight_part, 'dp', scatter_dimension=1, tiled=True)  131 us
    all_gather x1, waiting for transfers between devices, shards(): gathered = lax.all_gather(local_rows, 'tensor', axis=0, tiled=True)  106 us
    all_gather x1, waiting for transfers between devices, shards(): full_weight = lax.all_gather(out_weight, 'dp', axis=1, tiled=True)  69.5 us
    dot_general x1, matrix products, shards(): jnp.einsum('sh,sd->hd', out_flat, gathered, preferred_element_type=jnp.fl...  12.5 us
    dot_general x1, matrix products, shards(): jnp.einsum('sd,hd->sh', gathered, full_weight, preferred_element_type=jnp...  11.5 us
  transfers between devices with their start and end apart: 5, of which 3 were waited for; matrix products, arithmetic and copies ran while one was open for 6% of the time, Pallas kernels for 0%

commit v1 on v0

--- a/solution.py
+++ b/solution.py
@@ -4,6 +4,16 @@
 from jax.sharding import PartitionSpec as P
 
 HEAD_SIZE = 128
+
+
+def turned_line(x, mesh_axis, d):
+    devices = lax.axis_size(mesh_axis)
+    held, shards = (x, [x])
+    for _ in range(devices - 1):
+        held = lax.ppermute(held, mesh_axis, [(i, (i + 1) % devices) for i in range(devices)])
+        shards.insert(0, held)
+    line = jnp.concatenate(shards, axis=d)
+    return jnp.roll(line, (lax.axis_index(mesh_axis) + 1) * x.shape[d], axis=d)
 
 
 def swapped(value, axis, apart):
@@ -27,7 +37,7 @@
     doc_ids = jnp.sum((positions[:, None] >= doc_ends[None, :]).astype(jnp.int32), axis=1)
     block_rows = min(512, seq_len)
     block_count = seq_len // block_rows
-    full_weight = lax.all_gather(out_weight, "dp", axis=1, tiled=True)
+    full_weight = turned_line(out_weight, "dp", 1)
 
     def key_reach():
         return seq_len

time: 375 us -> 310 us (0.83)
  waiting for transfers between devices: 308 us -> 214 us
  local copies, waits for them, and re-layouts: 3.8 us -> 24.5 us
  matrix products: 42.1 us -> 46.9 us
    all_gather x1, waiting for transfers between devices: 106 us -> 0.01 us  [shards(): gathered = lax.all_gather(local_rows, 'tensor', axis=0, tiled=True)]
    ppermute x0 -> x7, waiting for transfers between devices: none -> 86.5 us  [turned_line(): lax.ppermute(held, mesh_axis, [(i, (i + 1) % devices) for i in range(devi...]
    all_gather x1 -> x0, waiting for transfers between devices: 69.5 us -> none  [shards(): full_weight = lax.all_gather(out_weight, 'dp', axis=1, tiled=True)]
    unnamed x24 -> x57, local copies, waits for them, and re-layouts: 2.76 us -> 21.9 us
    reduce_scatter x1, waiting for transfers between devices: 131 us -> 127 us  [shards(): lax.psum_scatter(weight_part, 'dp', scatter_dimension=1, tiled=True)]
  transfers between devices with their start and end apart: 5 -> 11, of which waited for: 3 -> 8; matrix products, arithmetic and copies ran while one was open for 6% -> 15% of each run, Pallas kernels for 0% -> 0%
where the time goes in v1:
time: 310 us; the launch traced here: 309 us
  waiting for transfers between devices  214 us (69%)
  matrix products  46.9 us (15%)
  local copies, waits for them, and re-layouts  24.5 us (8%)
  between operations  14.5 us (5%)
  other arithmetic  5.53 us (2%)
  starting transfers between devices  3.23 us (1%)
    reduce_scatter x1, waiting for transfers between devices, shards(): lax.psum_scatter(weight_part, 'dp', scatter_dimension=1, tiled=True)  127 us
    ppermute x7, waiting for transfers between devices, turned_line(): lax.ppermute(held, mesh_axis, [(i, (i + 1) % devices) for i in range(devi...  86.5 us
    unnamed x57, local copies, waits for them, and re-layouts  21.9 us
    dot_general x1, matrix products, shards(): jnp.einsum('sh,sd->hd', out_flat, gathered, preferred_element_type=jnp.fl...  12.7 us
    dot_general x1, matrix products, shards(): jnp.einsum('sd,hd->sh', gathered, full_weight, preferred_element_type=jnp...  11.6 us
    dot_general x2, matrix products, shards(): jnp.einsum('hqk,kd->hqd', prob_bf16, value_rows, preferred_element_type=j...  7.6 us
  transfers between devices with their start and end apart: 11, of which 8 were waited for; matrix products, arithmetic and copies ran while one was open for 15% of the time, Pallas kernels for 0%

profile of v1, /device:TPU:0, one launch (start us, length us, event | category | flops | bytes accessed | tf_op | source)
XLA Modules:
  0.0 309.0 jit_solution(2205856693941327589)
XLA Ops:
  7.2 0.0 copy-start
  7.2 0.0 all-gather.3.cloned.1.call-start
  7.3 0.7 all-gather.3.cloned.1.call-update
  7.9 0.0 reduce-scatter.2.cloned.1.call-start
  8.0 0.3 copy-done.5
  8.3 3.0 collective-permute-start
  11.3 15.0 %collective-permute-done = bf16[256,1024]{1,0:T(8,128)(2,1)S(1)} collective-permute-done((bf16[256,1024]{1,0:T(8,128)(2,1)S(1)}, bf16[256,1024]{1,0:T(8,128)(2,1)S(1)}, u32[]{:S(2)}, u32[]{:S(2)}) %collective-permute-start) | collective-permute-done | bytes 524320 | tf_op jit(solution)/shard_map/ppermute | solution.py:13
  26.2 15.8 %collective-permute-done.1 = bf16[256,1024]{1,0:T(8,128)(2,1)S(1)} collective-permute-done((bf16[256,1024]{1,0:T(8,128)(2,1)S(1)}, bf16[256,1024]{1,0:T(8,128)(2,1)S(1)}, u32[]{:S(2)}, u32[]{:S(2)}) %collective-permute-start.1) | collective-permute-done | bytes 524320 | tf_op jit(solution)/shard_map/ppermute | solution.py:13
  42.0 0.2 reduce-window.8
  42.2 0.2 copy.29
  42.4 1.0 copy.30
  43.4 0.1 convert_reduce_fusion
  43.5 13.5 %collective-permute-done.2 = bf16[256,1024]{1,0:T(8,128)(2,1)} collective-permute-done((bf16[256,1024]{1,0:T(8,128)(2,1)S(1)}, bf16[256,1024]{1,0:T(8,128)(2,1)}, u32[]{:S(2)}, u32[]{:S(2)}) %collective-permute-start.2) | collective-permute-done | bytes 524320 | tf_op jit(solution)/shard_map/ppermute | solution.py:13
  57.1 0.9 fusion.10
  58.0 13.4 %collective-permute-done.3 = bf16[256,1024]{1,0:T(8,128)(2,1)S(1)} collective-permute-done((bf16[256,1024]{1,0:T(8,128)(2,1)}, bf16[256,1024]{1,0:T(8,128)(2,1)S(1)}, u32[]{:S(2)}, u32[]{:S(2)}) %collective-permute-start.3) | collective-permute-done | bytes 524320 | tf_op jit(solution)/shard_map/ppermute | solution.py:13
  71.3 2.1 fusion.7
  73.5 0.9 fusion.8
  74.5 10.1 %collective-permute-done.4 = bf16[256,1024]{1,0:T(8,128)(2,1)S(1)} collective-permute-done((bf16[256,1024]{1,0:T(8,128)(2,1)S(1)}, bf16[256,1024]{1,0:T(8,128)(2,1)S(1)}, u32[]{:S(2)}, u32[]{:S(2)}) %collective-permute-start.4) | collective-permute-done | bytes 524320 | tf_op jit(solution)/shard_map/ppermute | solution.py:13
  84.6 2.0 exponential_reduce_fusion
  86.6 10.4 %collective-permute-done.5 = bf16[256,1024]{1,0:T(8,128)(2,1)} collective-permute-done((bf16[256,1024]{1,0:T(8,128)(2,1)S(1)}, bf16[256,1024]{1,0:T(8,128)(2,1)}, u32[]{:S(2)}, u32[]{:S(2)}) %collective-permute-start.5) | collective-permute-done | bytes 524320 | tf_op jit(solution)/shard_map/ppermute | solution.py:13
  97.0 0.0 collective-permute-start.6
  97.1 0.0 copy-start.9
  97.1 3.8 %convolution_convert_fusion.1 = bf16[2,512,128]{2,1,0:T(8,128)(2,1)S(1)} fusion(bf16[1,1024,256]{2,1,0:T(8,128)(2,1)S(1)} %copy-done, s32[]{:T(128)S(6)} %select_n.45, f32[1024,2,512]{2,0,1:T(8,128)} %copy-done.3, f32[2,512]{1,0:T(2,128)S(1)} %log_add_fusion, pred[512,1024]{0,1:T(8,128)(4,1)S(1)} %get-tuple-element.94), kind=kOutput, calls=%fused_computation.29 | convolution fusion | flops 272760832 | bytes 5246980 | tf_op jit(solution)/shard_map/hqk,kd->hqd/dot_general | solution.py:66
  100.9 8.3 %collective-permute-done.6 = bf16[256,1024]{1,0:T(8,128)(2,1)} collective-permute-done((bf16[256,1024]{1,0:T(8,128)(2,1)}, bf16[256,1024]{1,0:T(8,128)(2,1)}, u32[]{:S(2)}, u32[]{:S(2)}) %collective-permute-start.6) | collective-permute-done | bytes 524320 | tf_op jit(solution)/shard_map/ppermute | solution.py:13
  109.2 1.9 constant_dynamic-update-slice_fusion.15
  111.1 1.9 constant_dynamic-update-slice_fusion.14
  113.0 0.9 constant_dynamic-update-slice_fusion.13
  113.9 0.9 constant_dynamic-update-slice_fusion.12
  114.8 1.9 constant_dynamic-update-slice_fusion.11
  116.7 0.8 constant_dynamic-update-slice_fusion.10
  117.5 0.8 constant_dynamic-update-slice_fusion.9
  118.3 0.9 constant_dynamic-update-slice_fusion.8
  119.2 1.9 constant_dynamic-update-slice_fusion.7
  121.1 1.9 constant_dynamic-update-slice_fusion.6
  123.0 0.8 constant_dynamic-update-slice_fusion.5
  123.9 0.8 constant_dynamic-update-slice_fusion.4
  124.7 1.9 constant_dynamic-update-slice_fusion.3
  126.6 0.8 constant_dynamic-update-slice_fusion.2
  127.4 0.8 constant_dynamic-update-slice_fusion.1
  128.2 0.9 constant_dynamic-update-slice_fusion
  129.1 11.6 %fusion.11 = bf16[256,1024]{1,0:T(8,128)(2,1)S(1)} fusion(bf16[1,1024,8192]{2,1,0:T(8,128)(2,1)} %all-gather.3.cloned.1.call-done, bf16[256,16384]{1,0:T(8,128)(2,1)} %constant_dynamic-update-slice_fusion, s32[]{:T(128)S(6)} %select_n.48), kind=kOutput, calls=%fused_computation.21 | convolution fusion | flops 4295229440 | bytes 21495812 | tf_op jit(solution)/shard_map/sd,hd->sh/dot_general | solution.py:75
  140.7 0.3 copy.31
  141.0 3.8 %multiply_reduce_fusion.1 = (f32[2,512]{1,0:T(2,128)S(1)}, f32[2,512]{1,0:T(2,128)S(1)}, bf16[2,512,128]{2,1,0:T(8,128)(2,1)S(1)}) fusion(bf16[2,1024,128]{2,1,0:T(8,128)(2,1)S(1)} %bitcast.101, bf16[2,512,128]{2,1,0:T(8,128)(2,1)S(1)} %convolution_convert_fusion.1, bf16[1,1024,256]{2,1,0:T(8,128)(2,1)S(1)} %copy-done, s32[]{:T(128)S(6)} %select_n.45, ...), kind=kOutput, calls=%fused_computation.35 | convolution fusion | flops 273807360 | bytes 6041604 | tf_op jit(solution)/shard_map/hqk,kd->hqd/dot_general | solution.py:66
  144.8 0.2 copy.39
  145.0 12.7 %fusion = f32[256,8192]{1,0:T(8,128)} fusion(bf16[1024,256]{0,1:T(8,128)(2,1)S(1)} %bitcast.94, bf16[1,1024,8192]{2,1,0:T(8,128)(2,1)} %all-gather.3.cloned.1.call-done), kind=kOutput, calls=%fused_computation | convolution fusion | flops 4294967296 | bytes 25690112 | tf_op jit(solution)/shard_map/sh,sd->hd/dot_general | solution.py:78
  157.7 0.0 reduce-scatter.2.cloned.1.call-update
  157.8 3.4 %convolution_bitcast_fusion = f32[1024,128]{1,0:T(8,128)S(1)} fusion(bf16[2,1024,128]{2,1,0:T(8,128)(2,1)S(1)} %bitcast.102, f32[1024,2,512]{2,0,1:T(8,128)} %copy-done.3, f32[2,512]{1,0:T(2,128)S(1)} %log_add_fusion, pred[512,1024]{0,1:T(8,128)(4,1)S(1)} %get-tuple-element.94), kind=kOutput, calls=%fused_computation.22 | convolution fusion | flops 272629760 | bytes 5509120 | tf_op jit(solution)/shard_map/hqk,hqd->kd/dot_general | solution.py:111
  161.2 0.1 copy-done.2
  161.2 1.3 fusion.17
  162.5 0.1 collective-permute-start.8
  162.6 1.3 copy-done.4
  163.9 2.7 multiply_convert_fusion
  166.6 0.7 convolution_bitcast_fusion.2
  167.3 0.0 copy-start.18
  167.3 1.7 multiply_convert_fusion.1
  169.1 0.8 convolution_convert_fusion.2
  169.8 0.7 fusion.16
  170.6 0.8 convolution_convert_fusion
  171.3 0.1 collective-permute-start.7
  171.5 0.2 copy.38
  171.7 1.0 copy.40
  172.7 1.6 fusion.45
  174.3 0.7 fusion.44
  175.0 127.2 %reduce-scatter.2.cloned.1.call-done = f32[256,1024]{1,0:T(8,128)} async-done(((f32[256,8192]{1,0:T(8,128)}), f32[256,1024]{1,0:T(8,128)}) %reduce-scatter.2.cloned.1.call-update) | async-done | bytes 1048592 | tf_op jit(solution)/shard_map/reduce_scatter | solution.py:79
  (53 shorter events, 0.3 us)
Async XLA Ops:
  7.2 89.9 %copy-start = (bf16[1,1024,256]{2,1,0:T(8,128)(2,1)S(1)}, bf16[1,1024,256]{2,1,0:T(8,128)(2,1)}, u32[]{:S(2)}) copy-start(bf16[1,1024,256]{2,1,0:T(8,128)(2,1)} %param.24) | copy-start | bytes 1572868
  7.2 1.1 copy-start.5
  7.2 34.8 %copy-start.19 = (s32[1,4]{1,0:T(1,128)S(1)}, s32[1,4]{1,0:T(1,128)}, u32[]{:S(2)}) copy-start(s32[1,4]{1,0:T(1,128)} %param.27) | copy-start | bytes 52
  7.2 35.0 %copy-start.14 = (bf16[1,1024,256]{2,1,0:T(8,128)(2,1)S(1)}, bf16[1,1024,256]{2,1,0:T(8,128)(2,1)}, u32[]{:S(2)}) copy-start(bf16[1,1024,256]{2,1,0:T(8,128)(2,1)} %param.22) | copy-start | bytes 1572868
  7.2 121.9 %all-gather.3.cloned.1.call-start = ((), (), s32[]{:S(2)}) async-start(), calls=%async_computation.2 | async-start | bytes 20971520 | tf_op jit(solution)/shard_map/all_gather | solution.py:74
  7.9 294.3 %reduce-scatter.2.cloned.1.call-start = ((), (), s32[]{:S(2)}) async-start(), calls=%async_computation.1 | async-start | bytes 9437184 | tf_op jit(solution)/shard_map/reduce_scatter | solution.py:79
  8.3 18.0 %collective-permute-start = (bf16[256,1024]{1,0:T(8,128)(2,1)S(1)}, bf16[256,1024]{1,0:T(8,128)(2,1)S(1)}, u32[]{:S(2)}, u32[]{:S(2)}) collective-permute-start(bf16[256,1024]{1,0:T(8,128)(2,1)S(1)} %copy-done.5), channel_id=1, source_target_pairs={{0,4},{4,8},{8,12},{12,16},{16,20},{20,24},{24,28},{28,0},{1,5},{5... | collective-permute-start | bytes 1572872 | tf_op jit(solution)/shard_map/ppermute | solution.py:13
  26.2 15.8 %collective-permute-start.1 = (bf16[256,1024]{1,0:T(8,128)(2,1)S(1)}, bf16[256,1024]{1,0:T(8,128)(2,1)S(1)}, u32[]{:S(2)}, u32[]{:S(2)}) collective-permute-start(bf16[256,1024]{1,0:T(8,128)(2,1)S(1)} %collective-permute-done), channel_id=1, source_target_pairs={{0,4},{4,8},{8,12},{12,16},{16,20},{20,24},{24,28},{28,0},{1,5},{5... | collective-permute-start | bytes 1572872 | tf_op jit(solution)/shard_map/ppermute | solution.py:13
  42.0 15.0 %collective-permute-start.2 = (bf16[256,1024]{1,0:T(8,128)(2,1)S(1)}, bf16[256,1024]{1,0:T(8,128)(2,1)}, u32[]{:S(2)}, u32[]{:S(2)}) collective-permute-start(bf16[256,1024]{1,0:T(8,128)(2,1)S(1)} %collective-permute-done.1), channel_id=1, source_target_pairs={{0,4},{4,8},{8,12},{12,16},{16,20},{20,24},{24,28},{28,0},{1,5},{5... | collective-permute-start | bytes 1572872 | tf_op jit(solution)/shard_map/ppermute | solution.py:13
  43.4 30.1 %copy-start.10 = (bf16[1024,2,128]{2,0,1:T(8,128)(2,1)S(1)}, bf16[1024,2,128]{2,0,1:T(8,128)(2,1)}, u32[]{:S(2)}) copy-start(bf16[1024,2,128]{2,0,1:T(8,128)(2,1)} %copy.30) | copy-start | bytes 1572868
  43.4 30.1 %copy-start.17 = (bf16[1,1024,256]{2,1,0:T(8,128)(2,1)S(1)}, bf16[1,1024,256]{2,1,0:T(8,128)(2,1)}, u32[]{:S(2)}) copy-start(bf16[1,1024,256]{2,1,0:T(8,128)(2,1)} %param.23) | copy-start | bytes 1572868
  57.1 14.3 %collective-permute-start.3 = (bf16[256,1024]{1,0:T(8,128)(2,1)}, bf16[256,1024]{1,0:T(8,128)(2,1)S(1)}, u32[]{:S(2)}, u32[]{:S(2)}) collective-permute-start(bf16[256,1024]{1,0:T(8,128)(2,1)} %collective-permute-done.2), channel_id=1, source_target_pairs={{0,4},{4,8},{8,12},{12,16},{16,20},{20,24},{24,28},{28,0},{1,5},{5... | collective-permute-start | bytes 1572872 | tf_op jit(solution)/shard_map/ppermute | solution.py:13
  71.3 3.1 %copy-start.6 = (bf16[256,1024]{1,0:T(8,128)(2,1)}, bf16[256,1024]{1,0:T(8,128)(2,1)S(1)}, u32[]{:S(2)}) copy-start(bf16[256,1024]{1,0:T(8,128)(2,1)S(1)} %collective-permute-done.3) | copy-start | bytes 1572868
  71.3 13.2 %collective-permute-start.4 = (bf16[256,1024]{1,0:T(8,128)(2,1)S(1)}, bf16[256,1024]{1,0:T(8,128)(2,1)S(1)}, u32[]{:S(2)}, u32[]{:S(2)}) collective-permute-start(bf16[256,1024]{1,0:T(8,128)(2,1)S(1)} %collective-permute-done.3), channel_id=1, source_target_pairs={{0,4},{4,8},{8,12},{12,16},{16,20},{20,24},{24,28},{28,0},{1,5},{5... | collective-permute-start | bytes 1572872 | tf_op jit(solution)/shard_map/ppermute | solution.py:13
  73.5 13.0 %copy-start.1 = (f32[1024,2,512]{2,0,1:T(8,128)}, f32[1024,2,512]{2,0,1:T(8,128)S(1)}, u32[]{:S(2)}) copy-start(f32[1024,2,512]{2,0,1:T(8,128)S(1)} %get-tuple-element.99) | copy-start | bytes 12582916
  74.5 12.1 %copy-start.3 = (f32[1024,2,512]{2,0,1:T(8,128)}, f32[1024,2,512]{2,0,1:T(8,128)S(1)}, u32[]{:S(2)}) copy-start(f32[1024,2,512]{2,0,1:T(8,128)S(1)} %get-tuple-element.101) | copy-start | bytes 12582916
  84.6 2.0 copy-start.8
  84.6 12.5 %collective-permute-start.5 = (bf16[256,1024]{1,0:T(8,128)(2,1)S(1)}, bf16[256,1024]{1,0:T(8,128)(2,1)}, u32[]{:S(2)}, u32[]{:S(2)}) collective-permute-start(bf16[256,1024]{1,0:T(8,128)(2,1)S(1)} %collective-permute-done.4), channel_id=1, source_target_pairs={{0,4},{4,8},{8,12},{12,16},{16,20},{20,24},{24,28},{28,0},{1,5},{5... | collective-permute-start | bytes 1572872 | tf_op jit(solution)/shard_map/ppermute | solution.py:13
  97.0 12.2 %collective-permute-start.6 = (bf16[256,1024]{1,0:T(8,128)(2,1)}, bf16[256,1024]{1,0:T(8,128)(2,1)}, u32[]{:S(2)}, u32[]{:S(2)}) collective-permute-start(bf16[256,1024]{1,0:T(8,128)(2,1)} %collective-permute-done.5), channel_id=1, source_target_pairs={{0,4},{4,8},{8,12},{12,16},{16,20},{20,24},{24,28},{28,0},{1,5},{5... | collective-permute-start | bytes 1572872 | tf_op jit(solution)/shard_map/ppermute | solution.py:13
  97.1 16.0 %copy-start.9 = (bf16[256,1024]{1,0:T(8,128)(2,1)S(1)}, bf16[256,1024]{1,0:T(8,128)(2,1)}, u32[]{:S(2)}) copy-start(bf16[256,1024]{1,0:T(8,128)(2,1)} %copy-done.8) | copy-start | bytes 1572868
  97.1 16.8 %copy-start.7 = (bf16[256,1024]{1,0:T(8,128)(2,1)S(1)}, bf16[256,1024]{1,0:T(8,128)(2,1)}, u32[]{:S(2)}) copy-start(bf16[256,1024]{1,0:T(8,128)(2,1)} %copy-done.6) | copy-start | bytes 1572868
  141.0 20.2 %copy-start.15 = (bf16[1024,2,128]{2,0,1:T(8,128)(2,1)}, bf16[1024,2,128]{2,0,1:T(8,128)(2,1)S(1)}, u32[]{:S(2)}) copy-start(bf16[1024,2,128]{2,0,1:T(8,128)(2,1)S(1)} %copy.31) | copy-start | bytes 1572868
  157.8 3.5 %copy-start.2 = (f32[1024,2,512]{2,0,1:T(8,128)S(1)}, f32[1024,2,512]{2,0,1:T(8,128)}, u32[]{:S(2)}) copy-start(f32[1024,2,512]{2,0,1:T(8,128)} %copy-done.1) | copy-start | bytes 12582916
  161.2 2.6 copy-start.4
  162.5 4.1 %copy-start.12 = (f32[1024,128]{1,0:T(8,128)}, f32[1024,128]{1,0:T(8,128)S(1)}, u32[]{:S(2)}) copy-start(f32[1024,128]{1,0:T(8,128)S(1)} %fusion.17) | copy-start | bytes 1572868
  162.5 10.2 %collective-permute-start.8 = (f32[512,128]{1,0:T(8,128)S(1)}, f32[512,128]{1,0:T(8,128)}, u32[]{:S(2)}, u32[]{:S(2)}) collective-permute-start(f32[512,128]{1,0:T(8,128)S(1)} %constant_dynamic-slice_fusion), channel_id=1, source_target_pairs={{0,1},{1,0},{2,3},{3,2},{4,5},{5,4},{6,7},{7,6},{8,9},{9,8},{10,11... | collective-permute-start | bytes 786440 | tf_op jit(solution)/shard_map/ppermute | solution.py:22
  163.9 2.7 copy-start.11
  163.9 3.5 %copy-start.16 = (bf16[1024,2,128]{2,0,1:T(8,128)(2,1)S(1)}, bf16[1024,2,128]{2,0,1:T(8,128)(2,1)}, u32[]{:S(2)}) copy-start(bf16[1024,2,128]{2,0,1:T(8,128)(2,1)} %copy-done.15) | copy-start | bytes 1572868
  167.3 1.7 copy-start.18
  169.8 2.9 copy-start.13
  171.3 3.0 collective-permute-start.7
Sparse Core Ops, SparseCore 0:
  9.6 108.6 all-gather.2
  157.9 144.2 reduce-scatter.1
